TPU v7x, 128 devices: a whole 4x4x4 slice. The times are simulated.
128 devices in a mesh: dp: 32 (over y, z, core), bn: 4 (over x).
Axes of the slice: x: 4, y: 4, z: 4, core: 2. Of those that a mesh axis runs over, the one named last changes fastest.
Arguments:
- key_feats: bfloat16 [1024, 12, 16, 2048], P(('dp', 'bn')), may hold values from -22 to 22
- clip_starts: int32 [1024], P(('dp', 'bn')), may hold values from 0 to 4
- shuffle: int32 [4, 32], P('bn'), may hold values from 0 to 31, each once within a row
- query_feats: bfloat16 [1024, 2048], P(('dp', 'bn')), may hold values from -6 to 6
- conv_time: bfloat16 [3, 2048, 512], replicated, may hold values from -0.078125 to 0.078125
- conv_space: bfloat16 [9, 512, 512], replicated, may hold values from -0.09375 to 0.09375
- conv_expand: bfloat16 [512, 2048], replicated, may hold values from -0.25 to 0.25
- gain_one: float32 [512], replicated, may hold values from 0.25 to 1.75
- shift_one: float32 [512], replicated, may hold values from -3 to 3
- gain_two: float32 [512], replicated, may hold values from 0.25 to 1.75
- shift_two: float32 [512], replicated, may hold values from -3 to 3
- gain_three: float32 [2048], replicated, may hold values from 0.25 to 1.75
- shift_three: float32 [2048], replicated, may hold values from -3 to 3
- w_key: bfloat16 [2048, 128], replicated, may hold values from -0.125 to 0.125
- w_query: bfloat16 [2048, 128], replicated, may hold values from -0.125 to 0.125
- queue: bfloat16 [16384, 128], replicated, may hold values from -6 to 6
Outputs:
- keys: bfloat16 [1024, 128], P(('dp', 'bn'))
- query_grad: float32 [2048, 128], replicated
Inputs may be any that keep to these rules, and one draw needn't show every extreme that they name: `shuffle`: each row is a permutation of 0 to 31.
All inputs are finite; a program needn't handle non-finite values.
Results may differ from a plain program's by a relative error of at most 0.0061.
Values may be sent and summed in bfloat16 or wider, within the bound.
A program may use at most 128 MiB of HBM per device.

v0:
```python
import jax
import jax.numpy as jnp
from jax import lax
from jax.sharding import PartitionSpec as P

FRAMES = 8
SIDE = 4
SHARPNESS_DIVISOR = 0.2
EPSILON = 1e-05


def pick_frames(features, starts):

    def single(clip_feats, first_frame):
        return lax.dynamic_slice_in_dim(clip_feats, first_frame, FRAMES, 0)

    return jax.vmap(single)(features, starts)


def time_conv(values, weights):
    padded = jnp.pad(values, ((0, 0), (1, 1), (0, 0), (0, 0)))
    length = values.shape[1]
    summed = jnp.zeros(values.shape[:3] + (weights.shape[2],), jnp.float32)
    for offset in range(3):
        summed = summed + jnp.einsum(
            "afsc,cd->afsd",
            padded[:, offset : offset + length],
            weights[offset],
            preferred_element_type=jnp.float32,
        )
    return summed


def space_conv(values, weights):
    square_grid = values.reshape(values.shape[0], values.shape[1], SIDE, SIDE, values.shape[3])
    padded = jnp.pad(square_grid, ((0, 0), (0, 0), (1, 1), (1, 1), (0, 0)))
    summed = jnp.zeros(
        (values.shape[0], values.shape[1], SIDE, SIDE, weights.shape[2]), jnp.float32
    )
    for row_shift in range(3):
        for col_shift in range(3):
            window = padded[:, :, row_shift : row_shift + SIDE, col_shift : col_shift + SIDE]
            summed = summed + jnp.einsum(
                "afhwc,cd->afhwd",
                window,
                weights[3 * row_shift + col_shift],
                preferred_element_type=jnp.float32,
            )
    return summed.reshape(values.shape[0], values.shape[1], SIDE * SIDE, weights.shape[2])


def batch_norm(values, total_sum, squares, row_count, gain_row, shift_row):
    center = total_sum / row_count
    spread = squares / row_count - center * center
    return (values - center) * (gain_row * lax.rsqrt(spread + EPSILON)) + shift_row


def encode(values, params, moments, row_count):
    (
        conv_time,
        conv_space,
        conv_expand,
        gain_one,
        shift_one,
        gain_two,
        shift_two,
        gain_three,
        shift_three,
        w_key,
    ) = params
    first_out = time_conv(values, conv_time)
    total_sum, squares = moments(first_out)
    act_one = jnp.maximum(
        batch_norm(first_out, total_sum, squares, row_count, gain_one, shift_one), 0.0
    ).astype(jnp.bfloat16)
    second = space_conv(act_one, conv_space)
    total_sum, squares = moments(second)
    act_two = jnp.maximum(
        batch_norm(second, total_sum, squares, row_count, gain_two, shift_two), 0.0
    ).astype(jnp.bfloat16)
    third_out = jnp.einsum(
        "afsc,cd->afsd", act_two, conv_expand, preferred_element_type=jnp.float32
    )
    total_sum, squares = moments(third_out)
    merged = jnp.maximum(
        batch_norm(third_out, total_sum, squares, row_count, gain_three, shift_three)
        + values.astype(jnp.float32),
        0.0,
    )
    pooled = jnp.mean(merged, axis=(1, 2)).astype(jnp.bfloat16)
    projected = jnp.dot(pooled, w_key, preferred_element_type=jnp.float32)
    return (
        projected * lax.rsqrt(jnp.sum(projected * projected, axis=-1, keepdims=True) + 1e-06)
    ).astype(jnp.bfloat16)


def query_terms(query_feats, own_keys, w_query, queue):
    projected = jnp.dot(query_feats, w_query, preferred_element_type=jnp.float32)
    length = jnp.sqrt(jnp.sum(projected * projected, axis=-1, keepdims=True) + 1e-06)
    anchor_direction = projected / length
    queue_wide = queue.astype(jnp.float32)
    memory_bank_directions = (
        queue_wide * lax.rsqrt(jnp.sum(queue_wide * queue_wide, axis=-1, keepdims=True) + 1e-06)
    ).astype(jnp.bfloat16)
    collected_encodings = own_keys.astype(jnp.float32)
    matching_scores = jnp.sum(anchor_direction * collected_encodings, axis=-1) / SHARPNESS_DIVISOR
    distractor_scores = (
        jnp.einsum(
            "nf,ef->ne",
            anchor_direction.astype(jnp.bfloat16),
            memory_bank_directions,
            preferred_element_type=jnp.float32,
        )
        / SHARPNESS_DIVISOR
    )
    partition = jnp.exp(matching_scores) + jnp.sum(jnp.exp(distractor_scores), axis=-1)
    log_total = jnp.log(partition)
    weight_pos = jnp.exp(matching_scores - log_total)
    weight_neg = jnp.exp(distractor_scores - log_total[:, None]).astype(jnp.bfloat16)
    retrieved_samples = (
        jnp.dot(weight_neg, memory_bank_directions, preferred_element_type=jnp.float32)
        + (weight_pos - 1.0)[:, None] * collected_encodings
    )
    anchor_loss_derivative = retrieved_samples / SHARPNESS_DIVISOR
    radial = jnp.sum(anchor_direction * anchor_loss_derivative, axis=-1, keepdims=True)
    return ((anchor_loss_derivative - radial * anchor_direction) / length).astype(jnp.bfloat16)


def local(
    key_feats,
    clip_starts,
    shuffle,
    query_feats,
    conv_time,
    conv_space,
    conv_expand,
    gain_one,
    shift_one,
    gain_two,
    shift_two,
    gain_three,
    shift_three,
    w_key,
    w_query,
    queue,
):
    params = (
        conv_time,
        conv_space,
        conv_expand,
        gain_one,
        shift_one,
        gain_two,
        shift_two,
        gain_three,
        shift_three,
        w_key,
    )
    chosen = pick_frames(key_feats, clip_starts)
    peer_count = lax.axis_size("dp")
    groups = lax.axis_size("bn")
    target = shuffle[0, lax.axis_index("dp")]
    row_count = groups * chosen.shape[0] * chosen.shape[1] * chosen.shape[2]
    slot = (jnp.arange(peer_count, dtype=jnp.int32) == target).astype(jnp.float32)

    def group_moments(values):
        sums = jnp.stack(
            [jnp.sum(values, axis=(0, 1, 2)), jnp.sum(values * values, axis=(0, 1, 2))]
        )
        table = lax.psum(slot[:, None, None] * sums[None], ("dp", "bn"))
        own = lax.dynamic_index_in_dim(table, target, 0, keepdims=False)
        return (own[0], own[1])

    own_keys = encode(chosen, params, group_moments, row_count)
    grad_proj = query_terms(query_feats, own_keys, w_query, queue)
    grad_part = jnp.einsum("nc,ne->ce", query_feats, grad_proj, preferred_element_type=jnp.float32)
    query_grad = lax.psum(grad_part, ("dp", "bn"))
    return (own_keys, query_grad)


def solution(mesh):
    placed = (
        P(("dp", "bn"), None, None, None),
        P(("dp", "bn")),
        P("bn", None),
        P(("dp", "bn"), None),
        P(),
        P(),
        P(),
        P(),
        P(),
        P(),
        P(),
        P(),
        P(),
        P(),
        P(),
        P(),
    )
    return jax.shard_map(
        local, mesh=mesh, in_specs=placed, out_specs=(P(("dp", "bn"), None), P()), check_vma=False
    )
```

profile of v0, /device:TPU:1, one launch (start us, length us, event | category | flops | bytes accessed | tf_op | source)
XLA Modules:
  0.0 665.7 jit_solution(5777000886677736291)
XLA Ops:
  7.2 6.7 %copy.18 = bf16[8,12,16,2048]{3,2,0,1:T(8,128)(2,1)} copy(bf16[8,12,16,2048]{3,2,1,0:T(8,128)(2,1)} %param.16) | data formatting | bytes 12582912 | tf_op args[0]
  14.0 5.6 gather_fusion
  19.5 6.7 %fusion.6 = f32[8,8,16,512]{3,2,1,0:T(8,128)} fusion(bf16[8,8,16,2048]{3,2,1,0:T(8,128)(2,1)} %gather_fusion, bf16[3,2048,512]{2,1,0:T(8,128)(2,1)} %param.20), kind=kOutput, calls=%fused_computation.13 | convolution fusion | flops 2147483648 | bytes 8388608 | tf_op jit(solution)/shard_map/afsc,cd->afsd/dot_general | solution.py:25
  26.2 5.2 fusion.8
  32.7 7.7 %fusion.75 = (f32[512]{0:T(512)S(1)}, f32[512]{0:T(512)S(1)}, f32[8,8,16,512]{3,2,1,0:T(8,128)}) fusion(bf16[8,8,16,2048]{3,2,1,0:T(8,128)(2,1)} %gather_fusion, bf16[3,2048,512]{2,1,0:T(8,128)(2,1)} %param.20, f32[8,8,16,512]{3,2,1,0:T(8,128)} %fusion.8, f32[8,8,16,512]{3,2,1,0:T(8,128)} %fusion.6), kind=kOutput, calls=%fused_computation.113 | convolution fusion | flops 1881668608 | bytes 12587008 | tf_op jit(solution)/shard_map/afsc,cd->afsd/dot_general | solution.py:25
  40.4 0.8 broadcast_multiply_fusion.2
  43.2 143.4 %all-reduce.8.cloned.1.call-done = f32[32,2,512]{2,1,0:T(2,128)} async-done(((f32[32,2,512]{2,1,0:T(2,128)}), f32[32,2,512]{2,1,0:T(2,128)}) %all-reduce.8.cloned.1.call-update) | async-done | bytes 131088 | tf_op jit(solution)/shard_map/psum | solution.py:170
  186.6 0.8 dynamic-slice_multiply_fusion.5
  187.4 2.1 maximum_convert_fusion
  190.1 1.8 fusion.34
  191.9 1.7 fusion.36
  193.7 1.7 fusion.38
  195.4 0.7 fusion.40
  196.1 0.7 fusion.42
  196.9 0.7 fusion.44
  197.6 0.7 fusion.46
  198.3 0.7 fusion.48
  199.0 2.6 fusion.74
  201.6 0.8 broadcast_multiply_fusion.1
  202.7 3.9 fusion
  206.6 135.4 %all-reduce.10.cloned.1.call-done = f32[32,2,512]{2,1,0:T(2,128)} async-done(((f32[32,2,512]{2,1,0:T(2,128)}), f32[32,2,512]{2,1,0:T(2,128)}) %all-reduce.10.cloned.1.call-update) | async-done | bytes 131088 | tf_op jit(solution)/shard_map/psum | solution.py:170
  342.0 0.8 dynamic-slice_multiply_fusion.3
  342.9 8.0 %fusion.73 = (f32[2048]{0:T(1024)S(1)}, f32[2048]{0:T(1024)S(1)}, f32[8,8,16,2048]{3,2,1,0:T(8,128)}) fusion(bf16[512,2048]{1,0:T(8,128)(2,1)S(1)} %copy-done, f32[8,8,16,512]{3,1,2,0:T(8,128)} %bitcast.149, f32[512]{0:T(512)S(1)} %copy-done.12, f32[512]{0:T(512)S(1)} %rsqrt_multiply_fusion.1, f32[512]{0:T(512)S(1)} %bitcast.160), kind=kOutput, calls=%fused_computation.111 | convolution fusion | flops 2156392448 | bytes 12605440 | tf_op jit(solution)/shard_map/afsc,cd->afsd/dot_general | solution.py:81
  350.9 1.0 broadcast_multiply_fusion
  352.3 143.8 %all-reduce.12.cloned.1.call-done = f32[32,2,2048]{2,1,0:T(2,128)} async-done(((f32[32,2,2048]{2,1,0:T(2,128)}), f32[32,2,2048]{2,1,0:T(2,128)}) %all-reduce.12.cloned.1.call-update) | async-done | bytes 524304 | tf_op jit(solution)/shard_map/psum | solution.py:170
  496.1 0.8 dynamic-slice_multiply_fusion.1
  496.9 5.8 maximum_reduce_fusion
  503.1 2.5 exponential_reduce_fusion
  505.8 2.5 multiply_reduce_fusion.3
  508.3 1.4 convolution_bitcast_fusion
  509.7 147.0 %all-reduce.14.cloned.1.call-done = f32[2048,128]{0,1:T(8,128)} async-done(((f32[2048,128]{0,1:T(8,128)}), f32[2048,128]{0,1:T(8,128)}) %all-reduce.14.cloned.1.call-update) | async-done | bytes 1048592 | tf_op jit(solution)/shard_map/psum | solution.py:177
  656.7 2.5 copy.22
  (59 shorter events, 3.2 us)
Async XLA Ops:
  7.2 335.6 %copy-start = (bf16[512,2048]{1,0:T(8,128)(2,1)S(1)}, bf16[512,2048]{1,0:T(8,128)(2,1)}, u32[]{:S(2)}) copy-start(bf16[512,2048]{1,0:T(8,128)(2,1)} %param.22) | copy-start | bytes 6291460
  7.2 6.8 %copy-start.13 = (s32[8]{0:T(128)S(1)}, s32[8]{0:T(128)}, u32[]{:S(2)}) copy-start(s32[8]{0:T(128)} %param.17) | copy-start | bytes 100
  7.2 179.4 %all-reduce.8.cloned.1.call-start = ((), (), s32[]{:S(2)}) async-start(), calls=%async_computation | async-start | bytes 262144 | tf_op jit(solution)/shard_map/psum | solution.py:170
  19.5 6.7 %copy-start.2 = (bf16[8,8,16,2048]{3,2,1,0:T(8,128)(2,1)S(1)}, bf16[8,8,16,2048]{3,2,1,0:T(8,128)(2,1)}, u32[]{:S(2)}) copy-start(bf16[8,8,16,2048]{3,2,1,0:T(8,128)(2,1)} %gather_fusion) | copy-start | bytes 12582916
  26.2 5.2 copy-start.14
  32.7 154.6 %copy-start.8 = (f32[512]{0:T(512)S(1)}, f32[512]{0:T(512)}, u32[]{:S(2)}) copy-start(f32[512]{0:T(512)} %param.23) | copy-start | bytes 6148
  32.7 154.6 %copy-start.11 = (f32[512]{0:T(512)S(1)}, f32[512]{0:T(512)}, u32[]{:S(2)}) copy-start(f32[512]{0:T(512)} %param.24) | copy-start | bytes 6148
  41.2 300.9 %all-reduce.10.cloned.1.call-start = ((), (), s32[]{:S(2)}) async-start(), calls=%async_computation.1 | async-start | bytes 262144 | tf_op jit(solution)/shard_map/psum | solution.py:170
  187.3 8.1 %slice-start = ((s8[4718592]{0:T(1024)(128)(4,1)}), s8[4194304]{0:T(1024)(128)(4,1)S(1)}, s32[]{:S(2)}) async-start(s8[4718592]{0:T(1024)(128)(4,1)} %bitcast.147), calls=%async_computation.4 | async-start | bytes 8388608
  190.1 5.3 slice-start.1
  202.4 140.4 %copy-start.9 = (f32[512]{0:T(512)S(1)}, f32[512]{0:T(512)}, u32[]{:S(2)}) copy-start(f32[512]{0:T(512)} %param.25) | copy-start | bytes 6148
  202.4 140.4 %copy-start.12 = (f32[512]{0:T(512)S(1)}, f32[512]{0:T(512)}, u32[]{:S(2)}) copy-start(f32[512]{0:T(512)} %param.26) | copy-start | bytes 6148
  202.4 293.6 %all-reduce.12.cloned.1.call-start = ((), (), s32[]{:S(2)}) async-start(), calls=%async_computation.2 | async-start | bytes 1048576 | tf_op jit(solution)/shard_map/psum | solution.py:170
  342.8 9.2 %copy-start.3 = (bf16[2048,128]{1,0:T(8,128)(2,1)S(1)}, bf16[2048,128]{1,0:T(8,128)(2,1)}, u32[]{:S(2)}) copy-start(bf16[2048,128]{1,0:T(8,128)(2,1)} %param.30) | copy-start | bytes 1572868
  342.8 9.2 %copy-start.5 = (bf16[8,2048]{1,0:T(8,128)(2,1)S(1)}, bf16[8,2048]{1,0:T(8,128)(2,1)}, u32[]{:S(2)}) copy-start(bf16[8,2048]{1,0:T(8,128)(2,1)} %param.19) | copy-start | bytes 98308
  342.9 154.0 %copy-start.6 = (f32[2048]{0:T(1024)S(1)}, f32[2048]{0:T(1024)}, u32[]{:S(2)}) copy-start(f32[2048]{0:T(1024)} %param.27) | copy-start | bytes 24580
  342.9 154.0 %copy-start.7 = (f32[2048]{0:T(1024)S(1)}, f32[2048]{0:T(1024)}, u32[]{:S(2)}) copy-start(f32[2048]{0:T(1024)} %param.28) | copy-start | bytes 24580
  351.9 304.8 %all-reduce.14.cloned.1.call-start = ((), (), s32[]{:S(2)}) async-start(), calls=%async_computation.3 | async-start | bytes 2097152 | tf_op jit(solution)/shard_map/psum | solution.py:177
  496.9 5.9 copy-start.4
  496.9 6.2 copy-start.1
  505.8 2.5 copy-start.10
Sparse Core Ops, SparseCore 0:
  41.3 145.2 all-reduce.7
  202.5 139.4 all-reduce.9
  352.1 143.9 all-reduce.11
  509.8 146.8 all-reduce.13
where the time goes:
time: 666 us
  waiting for transfers between devices  570 us (86%)
  matrix products  45.9 us (7%)
  other arithmetic  17.6 us (3%)
  local copies, waits for them, and re-layouts  16.1 us (2%)
  between operations  16.1 us (2%)
    psum x3, waiting for transfers between devices, group_moments(): table = lax.psum(slot[:, None, None] * sums[None], ('dp', 'bn'))  423 us
    psum x1, waiting for transfers between devices, local(): query_grad = lax.psum(grad_part, ('dp', 'bn'))  147 us
    dot_general x3, matrix products, time_conv(): jnp.einsum('afsc,cd->afsd', padded[:, offset:offset + length], weights[of...  19.6 us
  transfers between devices with their start and end apart: 4, of which 4 were waited for; matrix products, arithmetic and copies ran while one was open for 1% of the time, Pallas kernels for 0%

commit v1 on v0

--- a/solution.py
+++ b/solution.py
@@ -174,7 +174,7 @@
     own_keys = encode(chosen, params, group_moments, row_count)
     grad_proj = query_terms(query_feats, own_keys, w_query, queue)
     grad_part = jnp.einsum("nc,ne->ce", query_feats, grad_proj, preferred_element_type=jnp.float32)
-    query_grad = lax.psum(grad_part, ("dp", "bn"))
+    query_grad = lax.psum(lax.psum(grad_part, "bn"), "dp")
     return (own_keys, query_grad)
 
 

time: 666 us -> 674 us (1.012)
  waiting for transfers between devices: 570 us -> 577 us
    psum x1 -> x2, waiting for transfers between devices: 147 us -> 154 us  [local(): query_grad = lax.psum(lax.psum(grad_part, 'bn'), 'dp')]
  transfers between devices with their start and end apart: 4 -> 5, of which waited for: 4 -> 5; matrix products, arithmetic and copies ran while one was open for 1% -> 1% of each run, Pallas kernels for 0% -> 0%
where the time goes in v1:
time: 674 us; the launch traced here: 673 us
  waiting for transfers between devices  577 us (86%)
  matrix products  45.9 us (7%)
  other arithmetic  17.6 us (3%)
  local copies, waits for them, and re-layouts  16.1 us (2%)
  between operations  16.1 us (2%)
    psum x3, waiting for transfers between devices, group_moments(): table = lax.psum(slot[:, None, None] * sums[None], ('dp', 'bn'))  423 us
    psum x2, waiting for transfers between devices, local(): query_grad = lax.psum(lax.psum(grad_part, 'bn'), 'dp')  154 us
    dot_general x3, matrix products, time_conv(): jnp.einsum('afsc,cd->afsd', padded[:, offset:offset + length], weights[of...  19.6 us
  transfers between devices with their start and end apart: 5, of which 5 were waited for; matrix products, arithmetic and copies ran while one was open for 1% of the time, Pallas kernels for 0%

profile of v1, /device:TPU:1, one launch (start us, length us, event | category | flops | bytes accessed | tf_op | source)
XLA Modules:
  0.0 673.1 jit_solution(9411924003373527989)
XLA Ops:
  7.2 6.7 copy.18
  14.0 5.6 gather_fusion
  19.5 6.7 fusion.6
  26.2 5.2 fusion.8
  32.7 7.7 %fusion.75 = (f32[512]{0:T(512)S(1)}, f32[512]{0:T(512)S(1)}, f32[8,8,16,512]{3,2,1,0:T(8,128)}) fusion(bf16[8,8,16,2048]{3,2,1,0:T(8,128)(2,1)} %gather_fusion, bf16[3,2048,512]{2,1,0:T(8,128)(2,1)} %param.20, f32[8,8,16,512]{3,2,1,0:T(8,128)} %fusion.8, f32[8,8,16,512]{3,2,1,0:T(8,128)} %fusion.6), kind=kOutput, calls=%fused_computation.113 | convolution fusion | flops 1881668608 | bytes 12587008 | tf_op jit(solution)/shard_map/afsc,cd->afsd/dot_general | solution.py:25
  40.4 0.8 broadcast_multiply_fusion.2
  43.2 143.4 %all-reduce.9.cloned.1.call-done = f32[32,2,512]{2,1,0:T(2,128)} async-done(((f32[32,2,512]{2,1,0:T(2,128)}), f32[32,2,512]{2,1,0:T(2,128)}) %all-reduce.9.cloned.1.call-update) | async-done | bytes 131088 | tf_op jit(solution)/shard_map/psum | solution.py:170
  186.6 0.8 dynamic-slice_multiply_fusion.5
  187.4 2.1 maximum_convert_fusion
  190.1 1.8 fusion.34
  191.9 1.7 fusion.36
  193.7 1.7 fusion.38
  195.4 0.7 fusion.40
  196.1 0.7 fusion.42
  196.9 0.7 fusion.44
  198.3 0.7 fusion.48
  199.0 2.6 fusion.74
  201.6 0.8 broadcast_multiply_fusion.1
  202.7 3.9 fusion
  206.6 135.4 %all-reduce.11.cloned.1.call-done = f32[32,2,512]{2,1,0:T(2,128)} async-done(((f32[32,2,512]{2,1,0:T(2,128)}), f32[32,2,512]{2,1,0:T(2,128)}) %all-reduce.11.cloned.1.call-update) | async-done | bytes 131088 | tf_op jit(solution)/shard_map/psum | solution.py:170
  342.0 0.8 dynamic-slice_multiply_fusion.3
  342.9 8.0 %fusion.73 = (f32[2048]{0:T(1024)S(1)}, f32[2048]{0:T(1024)S(1)}, f32[8,8,16,2048]{3,2,1,0:T(8,128)}) fusion(bf16[512,2048]{1,0:T(8,128)(2,1)S(1)} %copy-done, f32[8,8,16,512]{3,1,2,0:T(8,128)} %bitcast.149, f32[512]{0:T(512)S(1)} %copy-done.12, f32[512]{0:T(512)S(1)} %rsqrt_multiply_fusion.1, f32[512]{0:T(512)S(1)} %bitcast.160), kind=kOutput, calls=%fused_computation.111 | convolution fusion | flops 2156392448 | bytes 12605440 | tf_op jit(solution)/shard_map/afsc,cd->afsd/dot_general | solution.py:81
  350.9 1.0 broadcast_multiply_fusion
  352.3 143.8 %all-reduce.13.cloned.1.call-done = f32[32,2,2048]{2,1,0:T(2,128)} async-done(((f32[32,2,2048]{2,1,0:T(2,128)}), f32[32,2,2048]{2,1,0:T(2,128)}) %all-reduce.13.cloned.1.call-update) | async-done | bytes 524304 | tf_op jit(solution)/shard_map/psum | solution.py:170
  496.1 0.8 dynamic-slice_multiply_fusion.1
  496.9 5.8 maximum_reduce_fusion
  503.1 2.5 exponential_reduce_fusion
  505.8 2.5 multiply_reduce_fusion.3
  508.3 1.4 convolution_bitcast_fusion
  509.7 42.8 %all-reduce.15.cloned.1.call-done = f32[2048,128]{0,1:T(8,128)} async-done(((f32[2048,128]{0,1:T(8,128)}), f32[2048,128]{0,1:T(8,128)}) %all-reduce.15.cloned.1.call-update) | async-done | bytes 1048592 | tf_op jit(solution)/shard_map/psum | solution.py:177
  552.5 111.5 %all-reduce.17.cloned.1.call-done = f32[2048,128]{0,1:T(8,128)} async-done(((f32[2048,128]{0,1:T(8,128)}), f32[2048,128]{0,1:T(8,128)}) %all-reduce.17.cloned.1.call-update) | async-done | bytes 1048592 | tf_op jit(solution)/shard_map/psum | solution.py:177
  664.0 2.5 copy.22
  (62 shorter events, 4.0 us)
Async XLA Ops:
  7.2 335.6 %copy-start = (bf16[512,2048]{1,0:T(8,128)(2,1)S(1)}, bf16[512,2048]{1,0:T(8,128)(2,1)}, u32[]{:S(2)}) copy-start(bf16[512,2048]{1,0:T(8,128)(2,1)} %param.22) | copy-start | bytes 6291460
  7.2 6.8 %copy-start.13 = (s32[8]{0:T(128)S(1)}, s32[8]{0:T(128)}, u32[]{:S(2)}) copy-start(s32[8]{0:T(128)} %param.17) | copy-start | bytes 100
  7.2 179.4 %all-reduce.9.cloned.1.call-start = ((), (), s32[]{:S(2)}) async-start(), calls=%async_computation | async-start | bytes 262144 | tf_op jit(solution)/shard_map/psum | solution.py:170
  19.5 6.7 copy-start.2
  26.2 5.2 copy-start.14
  32.7 154.6 %copy-start.8 = (f32[512]{0:T(512)S(1)}, f32[512]{0:T(512)}, u32[]{:S(2)}) copy-start(f32[512]{0:T(512)} %param.23) | copy-start | bytes 6148
  32.7 154.6 %copy-start.11 = (f32[512]{0:T(512)S(1)}, f32[512]{0:T(512)}, u32[]{:S(2)}) copy-start(f32[512]{0:T(512)} %param.24) | copy-start | bytes 6148
  41.2 300.9 %all-reduce.11.cloned.1.call-start = ((), (), s32[]{:S(2)}) async-start(), calls=%async_computation.1 | async-start | bytes 262144 | tf_op jit(solution)/shard_map/psum | solution.py:170
  187.3 8.1 %slice-start = ((s8[4718592]{0:T(1024)(128)(4,1)}), s8[4194304]{0:T(1024)(128)(4,1)S(1)}, s32[]{:S(2)}) async-start(s8[4718592]{0:T(1024)(128)(4,1)} %bitcast.147), calls=%async_computation.5 | async-start | bytes 8388608
  190.1 5.3 slice-start.1
  202.4 140.4 %copy-start.9 = (f32[512]{0:T(512)S(1)}, f32[512]{0:T(512)}, u32[]{:S(2)}) copy-start(f32[512]{0:T(512)} %param.25) | copy-start | bytes 6148
  202.4 140.4 %copy-start.12 = (f32[512]{0:T(512)S(1)}, f32[512]{0:T(512)}, u32[]{:S(2)}) copy-start(f32[512]{0:T(512)} %param.26) | copy-start | bytes 6148
  202.4 293.6 %all-reduce.13.cloned.1.call-start = ((), (), s32[]{:S(2)}) async-start(), calls=%async_computation.2 | async-start | bytes 1048576 | tf_op jit(solution)/shard_map/psum | solution.py:170
  342.8 9.2 %copy-start.3 = (bf16[2048,128]{1,0:T(8,128)(2,1)S(1)}, bf16[2048,128]{1,0:T(8,128)(2,1)}, u32[]{:S(2)}) copy-start(bf16[2048,128]{1,0:T(8,128)(2,1)} %param.30) | copy-start | bytes 1572868
  342.8 9.2 %copy-start.5 = (bf16[8,2048]{1,0:T(8,128)(2,1)S(1)}, bf16[8,2048]{1,0:T(8,128)(2,1)}, u32[]{:S(2)}) copy-start(bf16[8,2048]{1,0:T(8,128)(2,1)} %param.19) | copy-start | bytes 98308
  342.9 154.0 %copy-start.6 = (f32[2048]{0:T(1024)S(1)}, f32[2048]{0:T(1024)}, u32[]{:S(2)}) copy-start(f32[2048]{0:T(1024)} %param.27) | copy-start | bytes 24580
  342.9 154.0 %copy-start.7 = (f32[2048]{0:T(1024)S(1)}, f32[2048]{0:T(1024)}, u32[]{:S(2)}) copy-start(f32[2048]{0:T(1024)} %param.28) | copy-start | bytes 24580
  351.9 200.6 %all-reduce.15.cloned.1.call-start = ((), (), s32[]{:S(2)}) async-start(), calls=%async_computation.3 | async-start | bytes 2097152 | tf_op jit(solution)/shard_map/psum | solution.py:177
  496.9 5.9 copy-start.4
  496.9 6.2 copy-start.1
  505.8 2.5 copy-start.10
  509.7 154.3 %all-reduce.17.cloned.1.call-start = ((), (), s32[]{:S(2)}) async-start(), calls=%async_computation.4 | async-start | bytes 2097152 | tf_op jit(solution)/shard_map/psum | solution.py:177
Sparse Core Ops, SparseCore 0:
  41.3 145.2 all-reduce.8
  202.5 139.4 all-reduce.10
  352.1 143.9 all-reduce.12
  509.8 42.6 all-reduce.14
  555.6 108.3 all-reduce.16
